TPU v7x, 256 devices: a whole 4x4x8 slice. The times are simulated.
256 devices in a mesh: row: 64 (over x, y_lo, z), panel: 4 (over y_hi, core).
Axes of the slice: x: 4, y: 4 (y_hi: 2, y_lo: 2; y = y_hi * 2 + y_lo), z: 8, core: 2. Of those that a mesh axis runs over, the one named last changes fastest.
Arguments:
- pixel_ids: int32 [65536], P('row'), may hold values from 0 to 65535, each once
- quad_offsets: int32 [2, 16, 65536], P(None, None, 'row'), may hold values from 0 to 7
- prior_factor: float32 [65536, 2048], P('row', 'panel'), may hold values from -0.036 to 0.036, as said below
Outputs:
- panel_factor: float32 [65536, 1024], P(('row', 'panel'))
Inputs may be any that keep to these rules, and one draw needn't show every extreme that they name: `pixel_ids`: each pixel of the grid appears in exactly one row. `prior_factor`: schur[panel_index] is positive definite.
All inputs are finite; a program needn't handle non-finite values.
Results may differ from a plain program's by a relative error of at most 0.0003.
Values sent between devices are 32-bit elements; how exact they have to be, the bound alone decides.
A program may use at most 128 MiB of HBM per device.

v0:
```python
import jax
import jax.numpy as jnp
from jax import lax
from jax.sharding import PartitionSpec as P

B = 1024
range_inverse = 1.0


def from_behind(block, axis, distance):
    devices = range(lax.axis_size(axis))
    route = [((i - distance) % len(devices), i) for i in devices]
    return lax.ppermute(block, axis, route)


def locate(pixel_ids, quad_offsets):
    column = (pixel_ids % 256).astype(jnp.float32)
    lines = (pixel_ids // 256).astype(jnp.float32)
    east = column[None, :] + (quad_offsets[0].astype(jnp.float32) + 0.5) / 8.0
    north = lines[None, :] + (quad_offsets[1].astype(jnp.float32) + 0.5) / 8.0
    return (east, north)


def cover_tile(east_rows, north_rows, east_cols, north_cols):
    count = east_rows.shape[0]

    def accumulate(index, running):
        east_one = lax.dynamic_index_in_dim(east_rows, index, 0, keepdims=False)
        north_one = lax.dynamic_index_in_dim(north_rows, index, 0, keepdims=False)
        apart_east = east_cols[:, :, None] - east_one[None, None, :]
        apart_north = north_cols[:, :, None] - north_one[None, None, :]
        return running + jnp.sum(
            jnp.exp(-(apart_east * apart_east + apart_north * apart_north) * range_inverse), axis=0
        )

    start = jnp.zeros((east_cols.shape[1], east_rows.shape[1]), jnp.float32)
    total = lax.fori_loop(0, count, accumulate, start)
    return total.T / float(count * count)


def local(pixel_ids, quad_offsets, prior_factor):
    panel_count = lax.axis_size("panel")
    row_count = lax.axis_size("row")
    block_rows = pixel_ids.shape[0]
    quarter_rows = block_rows // panel_count
    per_device = B // (row_count * panel_count)
    span_cols = panel_count * per_device
    row_pos = lax.axis_index("row")
    panel_pos = lax.axis_index("panel")
    east, north = locate(pixel_ids, quad_offsets)
    all_points = jnp.stack([east, north])
    own_points = lax.dynamic_slice_in_dim(all_points, panel_pos * quarter_rows, quarter_rows, 2)
    own_east = own_points[0]
    own_north = own_points[1]
    local_points = all_points.reshape(2, east.shape[0], panel_count, quarter_rows)[
        :, :, :, :per_device
    ]
    local_points = local_points.reshape(2, east.shape[0], span_cols)
    start_cols = jnp.zeros((quarter_rows, B), jnp.float32)

    def place(columns, held, source):
        tile = cover_tile(own_east, own_north, held[0], held[1])
        return lax.dynamic_update_slice(columns, tile, (jnp.int32(0), source * span_cols))

    def turn(index, carry):
        held, columns = carry
        columns = place(columns, held, (row_pos - index) % row_count)
        held = from_behind(held, "row", 1)
        return (held, columns)

    held, columns = lax.fori_loop(0, row_count - 1, turn, (local_points, start_cols))
    columns = place(columns, held, (row_pos - (row_count - 1)) % row_count)
    device_pos = row_pos * panel_count + panel_pos
    row_ids = jnp.arange(quarter_rows, dtype=jnp.int32)[:, None]
    col_ids = jnp.arange(B, dtype=jnp.int32)[None, :]
    on_diagonal = (row_ids < per_device) & (col_ids == device_pos * per_device + row_ids)
    cover = columns + jnp.where(on_diagonal, 1.0, 0.0).astype(jnp.float32)
    whole_rows = lax.all_to_all(prior_factor, "panel", split_axis=0, concat_axis=1, tiled=True)
    panel_prior = lax.all_gather(whole_rows[:per_device], ("row", "panel"), axis=0, tiled=True)
    update = jnp.dot(
        whole_rows,
        panel_prior.T,
        precision=lax.Precision.HIGHEST,
        preferred_element_type=jnp.float32,
    )
    schur = cover - update
    diag_rows = lax.all_gather(schur[:per_device], ("row", "panel"), axis=0, tiled=True)
    diag_factor = jnp.linalg.cholesky(diag_rows)
    return lax.linalg.triangular_solve(
        diag_factor, schur, left_side=False, lower=True, transpose_a=True
    )


def solution(mesh):
    return jax.shard_map(
        local,
        mesh=mesh,
        in_specs=(P("row"), P(None, None, "row"), P("row", "panel")),
        out_specs=P(("row", "panel"), None),
        check_vma=False,
    )
```

profile of v0, /device:TPU:32, one launch (start us, length us, event | category | flops | bytes accessed | tf_op | source)
XLA Modules:
  0.0 1338.7 jit_solution(4955843680710674743)
XLA Ops:
  11.4 26.9 %all-to-all-done = f32[4,256,512]{2,1,0:T(8,128)S(1)} async-done(((f32[4,256,512]{2,1,0:T(8,128)}), f32[4,256,512]{2,1,0:T(8,128)S(1)}, u32[]{:S(2)}, u32[]{:S(2)}) %all-to-all-start) | async-done | bytes 2097184 | tf_op jit(solution)/shard_map/all_to_all | solution.py:78
  39.1 497.6 %while.68 = (s32[]{:T(128)}, f32[2,16,16]{2,1,0:T(8,128)S(1)}, f32[256,1024]{0,1:T(8,128)S(1)}, f32[16,256]{1,0:T(8,128)S(1)}, f32[16,256]{1,0:T(8,128)S(1)}, /*...) while((s32[]{:T(128)}, f32[2,16,16]{2,1,0:T(8,128)S(1)}, ...), condition=%wide.region_4.5_spmd, body=%wide.region_0.4_spmd.sunk | while | flops 466965 | bytes 123403 | solution.py:71
  545.9 10.2 reshape.138
  556.0 16.1 %convolution_subtract_fusion = f32[256,1024]{1,0:T(8,128)S(1)} fusion(f32[256,2048]{0,1:T(8,128)S(1)} %bitcast.152, f32[1024,2048]{1,0:T(8,128)} %reshape.138, f32[256,1024]{1,0:T(8,128)S(1)} %dynamic_update_slice.13, s32[256]{0:T(256)S(1)} %iota_add_fusion, pred[256]{0:T(512)(128)(4,1)S(1)} %iota_compare_fusion.4), kind=kOutput, calls=%fused_computation.15 | convolution fusion | flops 6443761664 | bytes 12584192 | tf_op jit(solution)/shard_map/dot_general | solution.py:80
  573.7 412.5 %all-gather.7.cloned.1.call-done = f32[256,4,1024]{2,1,0:T(4,128)} async-done(((f32[1,4,1024]{2,1,0:T(4,128)}), f32[256,4,1024]{2,1,0:T(4,128)}) %all-gather.7.cloned.1.call-update) | async-done | bytes 4194320 | tf_op jit(solution)/shard_map/all_gather | solution.py:87
  986.2 5.3 reshape.140
  991.5 5.8 copy.69
  1003.6 11.7 cholesky.223
  1017.9 9.8 custom-call.62
  1031.6 11.9 cholesky.244
  1044.2 9.8 custom-call.63
  1057.3 11.7 cholesky.468
  1069.7 9.8 custom-call.64
  1083.0 11.9 cholesky.487
  1095.5 9.8 custom-call.65
  1108.8 11.7 cholesky.506
  1121.2 10.2 custom-call.66
  1134.7 11.7 cholesky.526
  1147.0 9.8 custom-call.67
  1159.8 11.7 cholesky.546
  1172.2 9.8 custom-call.68
  1184.6 11.7 cholesky.564
  1212.2 22.8 %while.69 = (s32[]{:T(128)}, f32[1024,1024]{1,0:T(8,128)}, s32[8,2]{0,1:T(2,128)S(1)}, f32[8,128,128]{2,1,0:T(8,128)S(1)}, s32[]{:T(128)}) while((s32[]{:T(128)}, f32[1024,1024]{1,0:T(8,128)}, s32[8,2]{0,1:T(2,128)S(1)}, f32[8,128,128]{2,1,0:T(8,128)S(1)}, s32[]{:T(128)}) %tuple.176), condition=%wide.while_cond, body=%wide.while_body.sunk | while | flops 2 | bytes 131189 | solution.py:89
  1235.1 78.8 %custom-call.69 = f32[8,128,128]{1,2,0:T(8,128)S(1)} custom-call(f32[8,128,128]{2,1,0:T(8,128)S(1)} %get-tuple-element.405), custom_call_target="InvertDiagBlocksLowerTriangular" | custom-call | tf_op jit(solution)/shard_map/triangular_solve | solution.py:89
  (3637 shorter events, 763.7 us)
Async XLA Ops:
  6.5 31.8 %all-to-all-start = ((f32[4,256,512]{2,1,0:T(8,128)}), f32[4,256,512]{2,1,0:T(8,128)S(1)}, u32[]{:S(2)}, u32[]{:S(2)}) async-start(f32[4,256,512]{2,1,0:T(8,128)} %bitcast.153), calls=%async_computation | async-start | bytes 4194304 | tf_op jit(solution)/shard_map/all_to_all | solution.py:78
  11.1 534.7 %all-gather.5.cloned.1.call-start = ((), (), s32[]{:S(2)}) async-start(), calls=%async_computation.1 | async-start | bytes 8421376 | tf_op jit(solution)/shard_map/all_gather | solution.py:79
  39.0 947.2 %all-gather.7.cloned.1.call-start = ((), (), s32[]{:S(2)}) async-start(), calls=%async_computation.2 | async-start | bytes 4210688 | tf_op jit(solution)/shard_map/all_gather | solution.py:87
  58.9 8.0 collective-permute-start
  66.8 8.0 collective-permute-start
  74.9 8.0 collective-permute-start
  82.9 8.1 collective-permute-start
  98.8 8.0 collective-permute-start
  114.8 8.0 collective-permute-start
  122.7 8.0 collective-permute-start
  130.7 8.0 collective-permute-start
  162.5 8.0 collective-permute-start
  186.4 8.0 collective-permute-start
  194.4 8.0 collective-permute-start
  218.3 8.0 collective-permute-start
  234.2 8.0 collective-permute-start
  250.1 8.0 collective-permute-start
  274.0 8.0 collective-permute-start
  305.8 8.0 collective-permute-start
  329.7 8.0 collective-permute-start
  345.6 8.0 collective-permute-start
  393.4 8.0 collective-permute-start
  465.1 8.0 collective-permute-start
  496.9 8.0 collective-permute-start
  (49 other events, 459.4 us)
Sparse Core Ops, SparseCore 0:
  39.1 420.7 all-gather.4
  573.8 412.3 all-gather.6
where the time goes:
time: 1350 us; the launch traced here: 1340 us
  waiting for transfers between devices  722 us (53%)
  other arithmetic  416 us (31%)
  local copies, waits for them, and re-layouts  69 us (5%)
  matrix products  55.5 us (4%)
  loops' own time  45.9 us (3%)
  between operations  19.1 us (1%)
    all_gather x1, waiting for transfers between devices, local(): lax.all_gather(schur[:per_device], ('row', 'panel'), axis=0, tiled=True)  412 us
    ppermute x63, waiting for transfers between devices, from_behind(): return lax.ppermute(block, axis, route)  283 us
    another operation x31, other arithmetic, local(): diag_factor = jnp.linalg.cholesky(diag_rows)  173 us
    reduce_sum x1024, other arithmetic, accumulate(): jnp.sum(jnp.exp(-(apart_east * apart_east + apart_north * apart_north) *...  148 us
    another operation x3, other arithmetic, local(): lax.linalg.triangular_solve(diag_factor, schur, left_side=False, lower=Tr...  83.7 us
    another operation x64, loops' own time, cover_tile(): total = lax.fori_loop(0, count, accumulate, start)  43 us
  transfers between devices with their start and end apart: 66, of which 64 were waited for; matrix products, arithmetic and copies ran while one was open for 13% of the time, Pallas kernels for 0%

commit v1 on v0

--- a/solution.py
+++ b/solution.py
@@ -75,7 +75,9 @@
     col_ids = jnp.arange(B, dtype=jnp.int32)[None, :]
     on_diagonal = (row_ids < per_device) & (col_ids == device_pos * per_device + row_ids)
     cover = columns + jnp.where(on_diagonal, 1.0, 0.0).astype(jnp.float32)
-    whole_rows = lax.all_to_all(prior_factor, "panel", split_axis=0, concat_axis=1, tiled=True)
+    shards = jnp.split(prior_factor, lax.axis_size("panel"), axis=0)
+    received = lax.all_to_all(jnp.stack(shards), "panel", 0, 0)
+    whole_rows = jnp.concatenate(received, axis=1)
     panel_prior = lax.all_gather(whole_rows[:per_device], ("row", "panel"), axis=0, tiled=True)
     update = jnp.dot(
         whole_rows,

time: 1350 us -> 1350 us (level)
    unnamed x18 -> x21, local copies, waits for them, and re-layouts: 25.7 us -> 27.3 us
where the time goes in v1:
time: 1350 us; the launch traced here: 1340 us
  waiting for transfers between devices  722 us (53%)
  other arithmetic  418 us (31%)
  local copies, waits for them, and re-layouts  69.9 us (5%)
  matrix products  55.5 us (4%)
  loops' own time  45.9 us (3%)
  between operations  19.1 us (1%)
    all_gather x1, waiting for transfers between devices, local(): lax.all_gather(schur[:per_device], ('row', 'panel'), axis=0, tiled=True)  412 us
    ppermute x63, waiting for transfers between devices, from_behind(): return lax.ppermute(block, axis, route)  283 us
    another operation x31, other arithmetic, local(): diag_factor = jnp.linalg.cholesky(diag_rows)  173 us
    reduce_sum x1024, other arithmetic, accumulate(): jnp.sum(jnp.exp(-(apart_east * apart_east + apart_north * apart_north) *...  148 us
    another operation x3, other arithmetic, local(): lax.linalg.triangular_solve(diag_factor, schur, left_side=False, lower=Tr...  83.7 us
    another operation x64, loops' own time, cover_tile(): total = lax.fori_loop(0, count, accumulate, start)  43 us
    unnamed x21, local copies, waits for them, and re-layouts  27.3 us
  transfers between devices with their start and end apart: 66, of which 64 were waited for; matrix products, arithmetic and copies ran while one was open for 13% of the time, Pallas kernels for 0%

profile of v1, /device:TPU:32, one launch (start us, length us, event | category | flops | bytes accessed | tf_op | source)
XLA Modules:
  0.0 1341.0 jit_solution(14373275677530595824)
XLA Ops:
  15.3 26.9 %all-to-all-done = f32[4,256,512]{1,2,0:T(8,128)S(1)} async-done(((f32[4,256,512]{1,2,0:T(8,128)}), f32[4,256,512]{1,2,0:T(8,128)S(1)}, u32[]{:S(2)}, u32[]{:S(2)}) %all-to-all-start) | async-done | bytes 2097184 | tf_op jit(solution)/shard_map/all_to_all | solution.py:79
  43.4 497.6 %while.68 = (s32[]{:T(128)}, f32[2,16,16]{2,1,0:T(8,128)S(1)}, f32[256,1024]{0,1:T(8,128)S(1)}, f32[16,256]{1,0:T(8,128)S(1)}, f32[16,256]{1,0:T(8,128)S(1)}, /*...) while((s32[]{:T(128)}, f32[2,16,16]{2,1,0:T(8,128)S(1)}, ...), condition=%wide.region_4.5_spmd, body=%wide.region_0.4_spmd.sunk | while | flops 466965 | bytes 123403 | solution.py:71
  548.3 10.0 reshape.143
  558.4 16.1 %convolution_subtract_fusion = f32[256,1024]{1,0:T(8,128)S(1)} fusion(f32[256,2048]{0,1:T(8,128)S(1)} %bitcast.155, f32[1024,2048]{1,0:T(8,128)} %reshape.143, f32[256,1024]{1,0:T(8,128)S(1)} %dynamic_update_slice.13, s32[256]{0:T(256)S(1)} %iota_add_fusion, pred[256]{0:T(512)(128)(4,1)S(1)} %iota_compare_fusion.4), kind=kOutput, calls=%fused_computation.16 | convolution fusion | flops 6443761664 | bytes 12584192 | tf_op jit(solution)/shard_map/dot_general | solution.py:82
  576.0 412.5 %all-gather.7.cloned.1.call-done = f32[256,4,1024]{2,1,0:T(4,128)} async-done(((f32[1,4,1024]{2,1,0:T(4,128)}), f32[256,4,1024]{2,1,0:T(4,128)}) %all-gather.7.cloned.1.call-update) | async-done | bytes 4194320 | tf_op jit(solution)/shard_map/all_gather | solution.py:89
  988.5 5.3 reshape.145
  993.8 5.8 copy.93
  1005.9 11.7 cholesky.223
  1020.2 9.8 custom-call.62
  1033.9 11.9 cholesky.244
  1046.5 9.8 custom-call.63
  1059.6 11.7 cholesky.468
  1072.0 9.8 custom-call.64
  1085.3 11.9 cholesky.487
  1097.8 9.8 custom-call.65
  1111.1 11.7 cholesky.506
  1123.5 10.2 custom-call.66
  1137.0 11.7 cholesky.526
  1149.3 9.8 custom-call.67
  1162.1 11.7 cholesky.546
  1174.5 9.8 custom-call.68
  1186.9 11.7 cholesky.564
  1214.5 22.8 %while.69 = (s32[]{:T(128)}, f32[1024,1024]{1,0:T(8,128)}, s32[8,2]{0,1:T(2,128)S(1)}, f32[8,128,128]{2,1,0:T(8,128)S(1)}, s32[]{:T(128)}) while((s32[]{:T(128)}, f32[1024,1024]{1,0:T(8,128)}, s32[8,2]{0,1:T(2,128)S(1)}, f32[8,128,128]{2,1,0:T(8,128)S(1)}, s32[]{:T(128)}) %tuple.179), condition=%wide.while_cond, body=%wide.while_body.sunk | while | flops 2 | bytes 131189 | solution.py:91
  1237.3 78.8 %custom-call.69 = f32[8,128,128]{1,2,0:T(8,128)S(1)} custom-call(f32[8,128,128]{2,1,0:T(8,128)S(1)} %get-tuple-element.405), custom_call_target="InvertDiagBlocksLowerTriangular" | custom-call | tf_op jit(solution)/shard_map/triangular_solve | solution.py:91
  (3641 shorter events, 766.1 us)
Async XLA Ops:
  10.6 31.7 %all-to-all-start = ((f32[4,256,512]{1,2,0:T(8,128)}), f32[4,256,512]{1,2,0:T(8,128)S(1)}, u32[]{:S(2)}, u32[]{:S(2)}) async-start(f32[4,256,512]{1,2,0:T(8,128)} %pad_maximum_fusion), calls=%async_computation | async-start | bytes 4194304 | tf_op jit(solution)/shard_map/all_to_all | solution.py:79
  15.0 533.3 %all-gather.5.cloned.1.call-start = ((), (), s32[]{:S(2)}) async-start(), calls=%async_computation.1 | async-start | bytes 8421376 | tf_op jit(solution)/shard_map/all_gather | solution.py:81
  43.3 945.2 %all-gather.7.cloned.1.call-start = ((), (), s32[]{:S(2)}) async-start(), calls=%async_computation.2 | async-start | bytes 4210688 | tf_op jit(solution)/shard_map/all_gather | solution.py:89
  55.2 8.0 collective-permute-start
  63.2 8.0 collective-permute-start
  71.1 8.0 collective-permute-start
  79.2 8.0 collective-permute-start
  87.2 8.1 collective-permute-start
  103.2 8.0 collective-permute-start
  119.1 8.0 collective-permute-start
  135.0 8.0 collective-permute-start
  166.8 8.0 collective-permute-start
  190.7 8.0 collective-permute-start
  198.7 8.0 collective-permute-start
  222.6 8.0 collective-permute-start
  238.5 8.0 collective-permute-start
  254.4 8.0 collective-permute-start
  278.3 8.0 collective-permute-start
  310.1 8.0 collective-permute-start
  334.0 8.0 collective-permute-start
  349.9 8.0 collective-permute-start
  397.7 8.0 collective-permute-start
  469.4 8.0 collective-permute-start
  501.2 8.0 collective-permute-start
  (48 other events, 452.1 us)
Sparse Core Ops, SparseCore 0:
  43.4 420.7 all-gather.4
  576.1 412.3 all-gather.6
